TPU v7x, 32 devices: a whole 2x2x4 slice. The times are simulated.
32 devices in a mesh: pole: 2 (over x), row: 8 (over z, y), col: 2 (over core).
Axes of the slice: x: 2, y: 2, z: 4, core: 2. Of those that a mesh axis runs over, the one named last changes fastest.
Arguments:
- panel: bfloat16 [4, 8, 2, 512, 128], P(('pole', 'col'), None, None, 'row'), parts along dimension 0, may hold values from -6 to 6
- tiles: bfloat16 [352, 2, 512, 512], P(('pole', 'row', 'col')), parts along dimension 0, may hold values from -0.078125 to 0.078125
- tile_slot: int32 [352], P(('pole', 'row', 'col')), parts along dimension 0, may hold values from 0 to 1
- tile_col: int32 [352], P(('pole', 'row', 'col')), parts along dimension 0, may hold values from 0 to 7
- pole_weight: float32 [4], P('pole'), parts along dimension 0, may hold values from -4 to 4
- box_orbitals: int32 [64, 256], P(('pole', 'row', 'col')), parts along dimension 0, may hold values from 0 to 8191, as said below
- box_basis: bfloat16 [64, 256, 512], P(('pole', 'row', 'col')), parts along dimension 0, may hold values from -0.375 to 0.375
- supernode_basis: bfloat16 [64, 128, 512], P(('pole', 'row', 'col')), parts along dimension 0, may hold values from -0.5 to 0.5
Outputs:
- inverse_column: float32 [32, 2, 512, 128], P(('pole', 'row'), None, 'col'), parts along dimension 0
- density: float32 [64, 512], P(('pole', 'row', 'col')), parts along dimension 0
There are 2 independent parts, one for each index of `pole`. A program takes and returns all parts, laid end to end along the dimension named above; each array names one. Nothing has to cross between parts.
Inputs may be any that keep to these rules, and one draw needn't show every extreme that they name: `box_orbitals`: let a row g be held by device r * 2 + c where r = (g // 512) // 2 and c = (g % 512) // (512 // 2). The 2 boxes of one device take at most 64 rows (counted with repeats) held by any one device, and exactly 64 from some device.
All inputs are finite; a program needn't handle non-finite values.
Results may differ from a plain program's by a relative error of at most 0.0029.
Values may be sent and summed in bfloat16 or wider, within the bound.
A program may use at most 64 MiB of HBM per device.

v0:
```python
import jax
import jax.numpy as jnp
from jax import lax
from jax.sharding import PartitionSpec as P

BR_DEV = 2


def local(panel, tiles, tile_slot, tile_col, pole_weight, box_orbitals, box_basis, supernode_basis):
    gathered = lax.all_gather(panel, "row", axis=3, tiled=True)
    blocks = gathered[0]
    selector = (tile_col[:, None] == jnp.arange(blocks.shape[0], dtype=jnp.int32)[None, :]).astype(
        jnp.bfloat16
    )
    chosen = jnp.einsum(
        "tj,jcbs->tcbs", selector, blocks, preferred_element_type=jnp.float32
    ).astype(jnp.bfloat16)
    real_part = jnp.einsum(
        "tab,tbs->tas", tiles[:, 0], chosen[:, 0], preferred_element_type=jnp.float32
    )
    real_part = real_part - jnp.einsum(
        "tab,tbs->tas", tiles[:, 1], chosen[:, 1], preferred_element_type=jnp.float32
    )
    imag_part = jnp.einsum(
        "tab,tbs->tas", tiles[:, 0], chosen[:, 1], preferred_element_type=jnp.float32
    )
    imag_part = imag_part + jnp.einsum(
        "tab,tbs->tas", tiles[:, 1], chosen[:, 0], preferred_element_type=jnp.float32
    )
    products = jnp.stack([real_part, imag_part], axis=1)
    partial_value = jnp.stack(
        [
            jnp.sum(jnp.where((tile_slot == slot_row)[:, None, None, None], products, 0.0), axis=0)
            for slot_row in range(BR_DEV)
        ]
    )
    summed = lax.psum_scatter(partial_value, "col", scatter_dimension=2, tiled=True)
    inverse_column = -summed
    density_local = (
        pole_weight[0] * inverse_column[:, 1] + pole_weight[1] * inverse_column[:, 0]
    ).astype(jnp.bfloat16)
    columns = density_local.shape[2]
    density_local = density_local.reshape(-1, columns)
    block_width = tiles.shape[2]
    col_count = lax.axis_size("col")
    half_rows = block_width // col_count
    wanted = box_orbitals.reshape(-1)
    wanted_total = wanted.shape[0]
    block_index = wanted // block_width
    within = wanted % block_width
    source = block_index // BR_DEV * col_count + within // half_rows
    local_row = block_index % BR_DEV * half_rows + within % half_rows
    start_rows = jnp.zeros((wanted_total, columns), jnp.bfloat16)
    shards = lax.all_gather(density_local[None], ("row", "col"), axis=0, tiled=True)
    count = shards.shape[0]
    inside = (source >= 0) & (source < count)
    clipped = jnp.clip(source, 0, count - 1)
    fetched = shards[clipped, local_row]
    picked = jnp.where(inside[:, None], fetched, start_rows)
    picked = picked.reshape(box_basis.shape[0], box_basis.shape[1], columns)
    projected = jnp.einsum("nas,nap->nsp", picked, box_basis, preferred_element_type=jnp.float32)
    density = jnp.sum(supernode_basis.astype(jnp.float32) * projected, axis=1)
    return (inverse_column, density)


def solution(mesh):
    return jax.shard_map(
        local,
        mesh=mesh,
        in_specs=(
            P(("pole", "col"), None, None, "row", None),
            P(("pole", "row", "col"), None, None, None),
            P(("pole", "row", "col")),
            P(("pole", "row", "col")),
            P("pole"),
            P(("pole", "row", "col"), None),
            P(("pole", "row", "col"), None, None),
            P(("pole", "row", "col"), None, None),
        ),
        out_specs=(P(("pole", "row"), None, "col", None), P(("pole", "row", "col"), None)),
        check_vma=False,
    )
```

profile of v0, /device:TPU:0, one launch (start us, length us, event | category | flops | bytes accessed | tf_op | source)
XLA Modules:
  0.0 160.1 jit_solution(1189421149225466076)
XLA Ops:
  7.2 1.9 %copy.27 = bf16[1,8,2,64,128]{4,1,3,2,0:T(8,128)(2,1)} copy(bf16[1,8,2,64,128]{4,3,2,1,0:T(8,128)(2,1)} %param.8) | data formatting | bytes 524288 | tf_op args[0]
  9.2 0.7 broadcast_compare_fusion
  9.8 52.7 %all-gather.3.cloned.1.call-done = bf16[1,8,2,512,128]{4,1,3,2,0:T(8,128)(2,1)} async-done(((bf16[1,8,2,64,128]{4,1,3,2,0:T(8,128)(2,1)}), bf16[1,8,2,512,128]{4,1,3,2,0:T(8,128)(2,1)}) %all-gather.3.cloned.1.call-update) | async-done | bytes 2097168 | tf_op jit(solution)/shard_map/all_gather | solution.py:10
  62.6 2.9 %convolution_convert_fusion = bf16[11,2,512,128]{3,0,2,1:T(8,128)(2,1)S(1)} fusion(bf16[1,8,2,512,128]{4,1,3,2,0:T(8,128)(2,1)} %all-gather.3.cloned.1.call-done, s32[11]{0:T(128)} %param.11), kind=kOutput, calls=%fused_computation.18 | convolution fusion | flops 24510552 | bytes 4980780 | tf_op jit(solution)/shard_map/tj,jcbs->tcbs/dot_general | solution.py:15
  65.5 2.7 %slice_bitcast_fusion = (bf16[11,512,128]{2,0,1:T(8,128)(2,1)}, bf16[11,512,128]{2,0,1:T(8,128)(2,1)}) fusion(bf16[11,2,512,128]{3,0,2,1:T(8,128)(2,1)S(1)} %convolution_convert_fusion), kind=kLoop, calls=%fused_computation.19 | loop fusion | bytes 5767168 | tf_op jit(solution)/shard_map/squeeze | solution.py:22
  68.2 3.2 %copy.31 = bf16[11,512,128]{1,2,0:T(8,128)(2,1)S(1)} copy(bf16[11,512,128]{2,0,1:T(8,128)(2,1)} %get-tuple-element.8) | data formatting | bytes 2883584 | tf_op jit(solution)/shard_map/squeeze | solution.py:22
  71.4 3.2 %copy.29 = bf16[11,512,128]{1,2,0:T(8,128)(2,1)S(1)} copy(bf16[11,512,128]{2,0,1:T(8,128)(2,1)} %get-tuple-element.9) | data formatting | bytes 2883584 | tf_op jit(solution)/shard_map/squeeze | solution.py:19
  74.6 4.6 %fusion.2 = f32[11,128,512]{2,1,0:T(8,128)S(1)} fusion(bf16[11,512,128]{1,2,0:T(8,128)(2,1)S(1)} %copy.31, bf16[11,2,512,512]{3,2,1,0:T(8,128)(2,1)} %param.9), kind=kOutput, calls=%fused_computation.4 | convolution fusion | flops 738197504 | bytes 10092544 | tf_op jit(solution)/shard_map/tab,tbs->tas/dot_general | solution.py:21
  79.3 4.8 %fusion = f32[11,128,512]{2,1,0:T(8,128)S(1)} fusion(bf16[11,512,128]{1,2,0:T(8,128)(2,1)S(1)} %copy.29, bf16[11,2,512,512]{3,2,1,0:T(8,128)(2,1)} %param.9), kind=kOutput, calls=%fused_computation.2 | convolution fusion | flops 738197504 | bytes 10092544 | tf_op jit(solution)/shard_map/tab,tbs->tas/dot_general | solution.py:27
  84.1 4.8 %subtract_bitcast_fusion = f32[11,1,512,128]{2,3,0,1:T(8,128)S(1)} fusion(f32[11,128,512]{2,1,0:T(8,128)S(1)} %fusion.2, bf16[11,512,128]{1,2,0:T(8,128)(2,1)S(1)} %copy.29, bf16[11,2,512,512]{3,2,1,0:T(8,128)(2,1)} %param.9), kind=kOutput, calls=%fused_computation.17 | convolution fusion | flops 738918400 | bytes 12976128 | tf_op jit(solution)/shard_map/tab,tbs->tas/dot_general | solution.py:18
  88.9 2.0 %add_bitcast_fusion = f32[11,1,512,128]{2,3,0,1:T(8,128)S(1)} fusion(f32[11,128,512]{2,1,0:T(8,128)S(1)} %fusion, bf16[11,512,128]{1,2,0:T(8,128)(2,1)S(1)} %copy.31, bf16[11,2,512,512]{3,2,1,0:T(8,128)(2,1)S(1)} %bitcast.55), kind=kOutput, calls=%fused_computation.16 | convolution fusion | flops 738918400 | bytes 12976128 | tf_op jit(solution)/shard_map/tab,tbs->tas/dot_general | solution.py:24
  90.9 1.0 select_reduce_fusion.1
  92.0 1.0 pad_maximum_fusion.1
  93.1 0.6 fusion.34
  93.7 6.5 %reduce-scatter.2.cloned.1.call-done = f32[2,2,256,128]{2,3,1,0:T(8,128)} async-done(((f32[2,2,512,128]{2,3,1,0:T(8,128)}), f32[2,2,256,128]{2,3,1,0:T(8,128)}) %reduce-scatter.2.cloned.1.call-update) | async-done | bytes 524304 | tf_op jit(solution)/shard_map/reduce_scatter | solution.py:37
  100.1 1.1 neg.3
  101.2 1.3 fusion.19
  102.6 0.8 copy.34
  103.4 0.1 fusion.29
  103.5 1.0 copy.36
  104.5 41.6 %all-gather.5.cloned.1.call-done = bf16[16,512,128]{2,1,0:T(8,128)(2,1)} async-done(((bf16[1,512,128]{2,1,0:T(8,128)(2,1)}), bf16[16,512,128]{2,1,0:T(8,128)(2,1)}) %all-gather.5.cloned.1.call-update) | async-done | bytes 2097168 | tf_op jit(solution)/shard_map/all_gather | solution.py:54
  146.1 6.4 %gather_fusion = bf16[512,128]{1,0:T(8,128)(2,1)S(1)} fusion(bf16[16,512,128]{2,1,0:T(8,128)(2,1)} %all-gather.5.cloned.1.call-done, s32[512]{0:T(512)S(1)} %bitcast.56), kind=kCustom, calls=%fused_computation | custom fusion | bytes 266240 | tf_op jit(solution)/shard_map/gather | solution.py:58
  152.6 0.1 copy.35
  152.7 0.8 fusion.17
  (23 shorter events, 0.2 us)
Async XLA Ops:
  7.2 145.5 %copy-start = (bf16[2,256,512]{2,1,0:T(8,128)(2,1)S(1)}, bf16[2,256,512]{2,1,0:T(8,128)(2,1)}, u32[]{:S(2)}) copy-start(bf16[2,256,512]{2,1,0:T(8,128)(2,1)} %param.14) | copy-start | bytes 1572868
  7.2 55.4 %all-gather.3.cloned.1.call-start = ((), (), s32[]{:S(2)}) async-start(), calls=%async_computation.1 | async-start | bytes 2359296 | tf_op jit(solution)/shard_map/all_gather | solution.py:10
  9.1 91.0 %reduce-scatter.2.cloned.1.call-start = ((), (), s32[]{:S(2)}) async-start(), calls=%async_computation.2 | async-start | bytes 1572864 | tf_op jit(solution)/shard_map/reduce_scatter | solution.py:37
  79.3 9.6 %slice-start = ((s8[11534336]{0:T(1024)(128)(4,1)}), s8[4194304]{0:T(1024)(128)(4,1)S(1)}, s32[]{:S(2)}) async-start(s8[11534336]{0:T(1024)(128)(4,1)} %bitcast.54), calls=%async_computation.4 | async-start | bytes 8388608
  79.3 9.6 %slice-start.1 = ((s8[11534336]{0:T(1024)(128)(4,1)}), s8[4194304]{0:T(1024)(128)(4,1)S(1)}, s32[]{:S(2)}) async-start(s8[11534336]{0:T(1024)(128)(4,1)} %bitcast.54), calls=%async_computation.5 | async-start | bytes 8388608
  84.0 4.9 %slice-start.2 = ((s8[11534336]{0:T(1024)(128)(4,1)}), s8[3145728]{0:T(1024)(128)(4,1)S(1)}, s32[]{:S(2)}) async-start(s8[11534336]{0:T(1024)(128)(4,1)} %bitcast.54), calls=%async_computation.6 | async-start | bytes 6291456
  92.0 1.1 copy-start.2
  92.0 11.4 %copy-start.1 = (s32[2,256]{1,0:T(2,128)S(1)}, s32[2,256]{1,0:T(2,128)}, u32[]{:S(2)}) copy-start(s32[2,256]{1,0:T(2,128)} %param.13) | copy-start | bytes 6148
  93.0 59.7 %copy-start.3 = (bf16[2,128,512]{2,1,0:T(8,128)(2,1)S(1)}, bf16[2,128,512]{2,1,0:T(8,128)(2,1)}, u32[]{:S(2)}) copy-start(bf16[2,128,512]{2,1,0:T(8,128)(2,1)} %param.15) | copy-start | bytes 786436
  93.0 53.1 %all-gather.5.cloned.1.call-start = ((), (), s32[]{:S(2)}) async-start(), calls=%async_computation.3 | async-start | bytes 2228224 | tf_op jit(solution)/shard_map/all_gather | solution.py:54
Sparse Core Ops, SparseCore 0:
  10.7 51.7 all-gather.2
  93.2 6.9 reduce-scatter.1
  103.5 42.6 all-gather.4
where the time goes:
time: 160 us
  waiting for transfers between devices  101 us (63%)
  local copies, waits for them, and re-layouts  20 us (12%)
  matrix products  19.9 us (12%)
  between operations  14 us (9%)
  other arithmetic  5.24 us (3%)
    all_gather x1, waiting for transfers between devices, local(): gathered = lax.all_gather(panel, 'row', axis=3, tiled=True)  52.7 us
    all_gather x1, waiting for transfers between devices, local(): lax.all_gather(density_local[None], ('row', 'col'), axis=0, tiled=True)  41.6 us
    gather x2, local copies, waits for them, and re-layouts, local(): fetched = shards[clipped, local_row]  6.54 us
    reduce_scatter x1, waiting for transfers between devices, local(): lax.psum_scatter(partial_value, 'col', scatter_dimension=2, tiled=True)  6.45 us
    squeeze x2, local copies, waits for them, and re-layouts, local(): chosen[:, 1]  5.91 us
    dot_general x1, matrix products, local(): jnp.einsum('tab,tbs->tas', tiles[:, 0], chosen[:, 0], preferred_element_t...  4.82 us
    dot_general x1, matrix products, local(): jnp.einsum('tab,tbs->tas', tiles[:, 1], chosen[:, 0], preferred_element_t...  4.75 us
    dot_general x1, matrix products, local(): jnp.einsum('tab,tbs->tas', tiles[:, 1], chosen[:, 1], preferred_element_t...  4.6 us
  transfers between devices with their start and end apart: 3, of which 3 were waited for; matrix products, arithmetic and copies ran while one was open for 1% of the time, Pallas kernels for 0%

commit v1 on v0

--- a/solution.py
+++ b/solution.py
@@ -1,12 +1,349 @@
+import functools
+
 import jax
 import jax.numpy as jnp
 from jax import lax
+from jax.experimental import pallas as pl
+from jax.experimental.pallas import tpu as pltpu
 from jax.sharding import PartitionSpec as P
 
 BR_DEV = 2
-
-
-def local(panel, tiles, tile_slot, tile_col, pole_weight, box_orbitals, box_basis, supernode_basis):
+MESH = pl.DeviceIdType.MESH
+
+
+def log2(value):
+    assert value & (value - 1) == 0
+    return value.bit_length() - 1
+
+
+def kernel(
+    rows, cols, slot_ref, tcol_ref, weight_ref, panel, tiles, orbitals, basis, super_basis,
+    inv_ref, density_ref, *scratch,
+):
+    lanes_y = 2
+    depth_z = rows // lanes_y
+    chunk_count = 2 * depth_z - 1
+    chunks = scratch[:chunk_count]
+    (tile_buf, basis_buf, super_buf, orb_buf, acc, half_in, pick_hot, basis_hot, send_rows, recv_rows,
+     local_sem, z_send, z_recv, y_send, y_recv, col_sem, orb_send, orb_recv, row_send, row_recv) = scratch[chunk_count:]
+    peers = rows * cols
+    r = lax.axis_index("row")
+    c = lax.axis_index("col")
+    me = r * cols + c
+    z = r // lanes_y
+    y = r % lanes_y
+    shard_rows = panel.shape[3]
+    width = panel.shape[4]
+    tile_count = tiles.shape[0]
+    block = tiles.shape[2]
+    half = block // cols
+    pair = lanes_y * shard_rows
+    boxes, orbs = orbitals.shape
+    capacity = send_rows.shape[1]
+
+    def spot(index):
+        return {"row": index // cols, "col": index % cols}
+
+    loads = [
+        pltpu.make_async_copy(panel.at[0], chunks[0].at[y], local_sem.at[0]),
+        pltpu.make_async_copy(tiles, tile_buf, local_sem.at[1]),
+        pltpu.make_async_copy(basis, basis_buf, local_sem.at[2]),
+        pltpu.make_async_copy(super_basis, super_buf, local_sem.at[3]),
+        pltpu.make_async_copy(orbitals, orb_buf.at[me], local_sem.at[4]),
+    ]
+    for load in loads:
+        load.start()
+    acc[...] = jnp.zeros_like(acc)
+
+    barrier = pltpu.get_barrier_semaphore()
+    for k in range(1, peers):
+        pl.semaphore_signal(barrier, inc=1, device_id=spot((me + k) % peers), device_id_type=MESH)
+    pl.semaphore_wait(barrier, peers - 1)
+
+    def up(d):
+        return d
+
+    def down(d):
+        return d if d == 0 else depth_z - 1 + d
+
+    def z_copy(kind, d, towards):
+        ident = up if kind == "up" else down
+        side = 0 if kind == "up" else 1
+        src = panel.at[0] if d == 0 else chunks[ident(d)].at[y]
+        return pltpu.make_async_remote_copy(
+            src_ref=src, dst_ref=chunks[ident(d + 1)].at[y],
+            send_sem=z_send.at[side, d], recv_sem=z_recv.at[side, d + 1],
+            device_id={"row": towards}, device_id_type=MESH,
+        )
+
+    def z_arrival(kind, d):
+        ident = up if kind == "up" else down
+        side = 0 if kind == "up" else 1
+        dst = chunks[ident(d)].at[y]
+        return pltpu.make_async_remote_copy(
+            src_ref=dst, dst_ref=dst, send_sem=z_send.at[side, d - 1], recv_sem=z_recv.at[side, d],
+            device_id={"row": r}, device_id_type=MESH,
+        )
+
+    other = r + 1 - 2 * y
+
+    def y_copy(ident):
+        src = panel.at[0] if ident == 0 else chunks[ident].at[y]
+        return pltpu.make_async_remote_copy(
+            src_ref=src, dst_ref=chunks[ident].at[y],
+            send_sem=y_send.at[ident], recv_sem=y_recv.at[ident],
+            device_id={"row": other}, device_id_type=MESH,
+        )
+
+    def y_arrival(ident):
+        dst = chunks[ident].at[1 - y]
+        return pltpu.make_async_remote_copy(
+            src_ref=dst, dst_ref=dst, send_sem=y_send.at[ident], recv_sem=y_recv.at[ident],
+            device_id={"row": other}, device_id_type=MESH,
+        )
+
+    def has(kind, d):
+        return z - d >= 0 if kind == "up" else z + d < depth_z
+
+    def can_send(kind):
+        return z + 1 < depth_z if kind == "up" else z >= 1
+
+    def next_row(kind):
+        return r + lanes_y if kind == "up" else r - lanes_y
+
+    def forward(kind, d):
+        @pl.when(jnp.logical_and(has(kind, d), can_send(kind)))
+        def _():
+            z_copy(kind, d, next_row(kind)).start()
+
+    def compute(ident, at_z):
+        offset = pl.multiple_of(at_z * pair, pair)
+        chunk = chunks[ident]
+
+        def one(t, carry):
+            j = tcol_ref[t]
+            slot = slot_ref[t]
+            left = jnp.concatenate(
+                [tile_buf[t, 0, :, pl.ds(offset, pair)], tile_buf[t, 1, :, pl.ds(offset, pair)]], axis=1)
+            parts = [chunk[k, j] for k in range(lanes_y)]
+            real = jnp.concatenate([p[0] for p in parts], axis=0)
+            imag = jnp.concatenate([p[1] for p in parts], axis=0)
+            right = jnp.concatenate(
+                [jnp.concatenate([real, imag], axis=1), jnp.concatenate([-imag, real], axis=1)], axis=0)
+            value = jnp.dot(left, right, preferred_element_type=jnp.float32)
+            for s in range(BR_DEV):
+                acc[s] += jnp.where(slot == s, value, 0.0)
+            return carry
+
+        lax.fori_loop(0, tile_count, one, 0)
+
+    forward("up", 0)
+    forward("down", 0)
+    y_copy(0).start()
+    orb_copies = []
+    for k in range(1, peers):
+        target = (me + k) % peers
+        orb_copies.append(pltpu.make_async_remote_copy(
+            src_ref=orbitals, dst_ref=orb_buf.at[me], send_sem=orb_send.at[k], recv_sem=orb_recv.at[k],
+            device_id=spot(target), device_id_type=MESH,
+        ))
+        orb_copies[-1].start()
+
+    loads[0].wait()
+
+    def prepare():
+        for k in range(1, peers):
+            origin = (me + peers - k) % peers
+            dst = orb_buf.at[origin]
+            pltpu.make_async_remote_copy(
+                src_ref=orbitals, dst_ref=dst, send_sem=orb_send.at[k], recv_sem=orb_recv.at[k],
+                device_id=spot(origin), device_id_type=MESH,
+            ).wait()
+        loads[4].wait()
+        loads[2].wait()
+        block_bits, half_bits = log2(block), log2(half)
+
+        def split(g):
+            row_block = g >> block_bits
+            within = g & (block - 1)
+            source = (row_block >> log2(BR_DEV)) * cols + (within >> half_bits)
+            local = (row_block & (BR_DEV - 1)) * half + (within & (half - 1))
+            return source, local
+
+        before = lax.broadcasted_iota(jnp.int32, (orbs, orbs), 0)
+        after = lax.broadcasted_iota(jnp.int32, (orbs, orbs), 1)
+        upper = jnp.where(before <= after, 1.0, 0.0).astype(jnp.bfloat16)
+
+        def ranks(masks):
+            seen = jnp.zeros((masks[0].shape[0], 1), jnp.float32)
+            result = []
+            for mask in masks:
+                counted = jnp.dot(mask.astype(jnp.bfloat16), upper, preferred_element_type=jnp.float32)
+                result.append(counted - 1.0 + seen)
+                seen = seen + jnp.sum(mask, axis=1, keepdims=True)
+            return result
+
+        asked = []
+        for n in range(boxes):
+            g = jnp.concatenate([orb_buf[q, n:n + 1, :] for q in range(peers)], axis=0)
+            source, local = split(g)
+            asked.append((jnp.where(source == me, 1.0, 0.0), local.astype(jnp.float32)))
+        order = ranks([a[0] for a in asked])
+        order = [jnp.where(a[0] > 0.5, o, -1.0) for a, o in zip(asked, order)]
+        place = lax.broadcasted_iota(jnp.int32, (capacity, orbs), 0).astype(jnp.float32)
+        row_id = lax.broadcasted_iota(jnp.int32, (capacity, BR_DEV * half), 1).astype(jnp.float32)
+        for q in range(peers):
+            found = jnp.zeros((capacity, 1), jnp.float32)
+            for n in range(boxes):
+                hit = place == order[n][q:q + 1]
+                found = found + jnp.sum(jnp.where(hit, asked[n][1][q:q + 1] + 1.0, 0.0), axis=1, keepdims=True)
+            pick_hot[q * capacity:(q + 1) * capacity, :] = jnp.where(
+                row_id == found - 1.0, 1.0, 0.0).astype(jnp.bfloat16)
+
+        masks = []
+        peer_id = lax.broadcasted_iota(jnp.int32, (peers, orbs), 0)
+        for n in range(boxes):
+            source, _ = split(orb_buf[me, n:n + 1, :])
+            masks.append(jnp.where(peer_id == source, 1.0, 0.0))
+        order = ranks(masks)
+        arrive = lax.broadcasted_iota(jnp.int32, (peers * capacity, orbs), 0).astype(jnp.float32)
+        for n in range(boxes):
+            position = jnp.sum(
+                masks[n] * (order[n] + (peer_id * capacity).astype(jnp.float32)), axis=0, keepdims=True)
+            hot = jnp.where(arrive == position, 1.0, 0.0).astype(jnp.bfloat16)
+            basis_hot[n] = jnp.dot(hot, basis_buf[n], preferred_element_type=jnp.float32).astype(jnp.bfloat16)
+
+    for d in range(1, depth_z + 1):
+        if d < depth_z:
+            for kind, ident in (("up", up(d)), ("down", down(d))):
+                @pl.when(has(kind, d))
+                def _(kind=kind, ident=ident):
+                    z_arrival(kind, d).wait_recv()
+                    y_copy(ident).start()
+                if d < depth_z - 1:
+                    forward(kind, d)
+        if d == 1:
+            y_arrival(0).wait_recv()
+            loads[1].wait()
+            compute(0, z)
+            prepare()
+        else:
+            for kind, ident, at_z in (("up", up(d - 1), z - d + 1), ("down", down(d - 1), z + d - 1)):
+                @pl.when(has(kind, d - 1))
+                def _(ident=ident, at_z=at_z):
+                    y_arrival(ident).wait_recv()
+                    compute(ident, at_z)
+
+    mine = pl.ds(pl.multiple_of(c * half, half), half)
+    theirs = pl.ds(pl.multiple_of((1 - c) * half, half), half)
+    swap = pltpu.make_async_remote_copy(
+        src_ref=acc.at[:, theirs, :], dst_ref=half_in, send_sem=col_sem.at[0], recv_sem=col_sem.at[1],
+        device_id={"col": 1 - c}, device_id_type=MESH,
+    )
+    swap.start()
+    swap.wait_recv()
+    density_rows = []
+    for s in range(BR_DEV):
+        column = -(acc[s, mine, :] + half_in[s])
+        real, imag = column[:, :width], column[:, width:]
+        inv_ref[s, 0] = real
+        inv_ref[s, 1] = imag
+        density_rows.append((weight_ref[0] * imag + weight_ref[1] * real).astype(jnp.bfloat16))
+    density_rows = jnp.concatenate(density_rows, axis=0)
+    picked = jnp.dot(pick_hot[...], density_rows, preferred_element_type=jnp.float32).astype(jnp.bfloat16)
+    send_rows[...] = picked.reshape(send_rows.shape)
+    row_copies = []
+    for k in range(1, peers):
+        target = (me + k) % peers
+        row_copies.append(pltpu.make_async_remote_copy(
+            src_ref=send_rows.at[target], dst_ref=recv_rows.at[me],
+            send_sem=row_send.at[k], recv_sem=row_recv.at[k],
+            device_id=spot(target), device_id_type=MESH,
+        ))
+        row_copies[-1].start()
+    recv_rows[me] = send_rows[me]
+    loads[3].wait()
+    for k in range(1, peers):
+        origin = (me + peers - k) % peers
+        dst = recv_rows.at[origin]
+        pltpu.make_async_remote_copy(
+            src_ref=dst, dst_ref=dst, send_sem=row_send.at[k], recv_sem=row_recv.at[k],
+            device_id=spot(origin), device_id_type=MESH,
+        ).wait_recv()
+    arrived = recv_rows[...].reshape(peers * capacity, width)
+    for n in range(boxes):
+        projected = lax.dot_general(
+            arrived, basis_hot[n], (((0,), (0,)), ((), ())), preferred_element_type=jnp.float32)
+        density_ref[n:n + 1, :] = jnp.sum(
+            super_buf[n].astype(jnp.float32) * projected, axis=0, keepdims=True)
+
+    for kind in ("up", "down"):
+        for d in range(depth_z - 1):
+            @pl.when(jnp.logical_and(has(kind, d), can_send(kind)))
+            def _(kind=kind, d=d):
+                z_copy(kind, d, next_row(kind)).wait_send()
+    y_copy(0).wait_send()
+    for d in range(1, depth_z):
+        for kind, ident in (("up", up(d)), ("down", down(d))):
+            @pl.when(has(kind, d))
+            def _(ident=ident):
+                y_copy(ident).wait_send()
+    swap.wait_send()
+    for copy in row_copies:
+        copy.wait_send()
+
+
+def fused(rows, cols, panel, tiles, tile_slot, tile_col, pole_weight, box_orbitals, box_basis, supernode_basis):
+    blocks, parts, shard_rows, width = panel.shape[1:]
+    tile_count, _, block, _ = tiles.shape
+    boxes, orbs = box_orbitals.shape
+    points = box_basis.shape[2]
+    half = block // cols
+    peers = rows * cols
+    capacity = 2 * boxes * orbs // peers
+    depth_z = rows // 2
+    dma = pltpu.SemaphoreType.DMA
+    bf16, f32 = jnp.bfloat16, jnp.float32
+    smem = pl.BlockSpec(memory_space=pltpu.SMEM)
+    hbm = pl.BlockSpec(memory_space=pl.ANY)
+    vmem = pl.BlockSpec(memory_space=pltpu.VMEM)
+    return pl.pallas_call(
+        functools.partial(kernel, rows, cols),
+        name="pole_step",
+        out_shape=(
+            jax.ShapeDtypeStruct((BR_DEV, 2, half, width), f32),
+            jax.ShapeDtypeStruct((boxes, points), f32),
+        ),
+        in_specs=[smem] * 3 + [hbm] * 5,
+        out_specs=(vmem, vmem),
+        scratch_shapes=[pltpu.VMEM((2, blocks, parts, shard_rows, width), bf16)] * (2 * depth_z - 1) + [
+            pltpu.VMEM(tiles.shape, bf16),
+            pltpu.VMEM(box_basis.shape, bf16),
+            pltpu.VMEM(supernode_basis.shape, bf16),
+            pltpu.VMEM((peers, boxes, orbs), jnp.int32),
+            pltpu.VMEM((BR_DEV, block, 2 * width), f32),
+            pltpu.VMEM((BR_DEV, half, 2 * width), f32),
+            pltpu.VMEM((peers * capacity, BR_DEV * half), bf16),
+            pltpu.VMEM((boxes, peers * capacity, points), bf16),
+            pltpu.VMEM((peers, capacity, width), bf16),
+            pltpu.VMEM((peers, capacity, width), bf16),
+            dma((5,)),
+            dma((2, depth_z)),
+            dma((2, depth_z)),
+            dma((2 * depth_z - 1,)),
+            dma((2 * depth_z - 1,)),
+            dma((2,)),
+            dma((peers,)),
+            dma((peers,)),
+            dma((peers,)),
+            dma((peers,)),
+        ],
+        compiler_params=pltpu.CompilerParams(
+            collective_id=0, has_side_effects=True, vmem_limit_bytes=56 * 1024 * 1024),
+    )(tile_slot, tile_col, pole_weight, panel, tiles, box_orbitals, box_basis, supernode_basis)
+
+
+def plain(panel, tiles, tile_slot, tile_col, pole_weight, box_orbitals, box_basis, supernode_basis):
     gathered = lax.all_gather(panel, "row", axis=3, tiled=True)
     blocks = gathered[0]
     selector = (tile_col[:, None] == jnp.arange(blocks.shape[0], dtype=jnp.int32)[None, :]).astype(
@@ -64,6 +401,13 @@
 
 
 def solution(mesh):
+    rows, cols = mesh.shape["row"], mesh.shape["col"]
+
+    def local(panel, *rest):
+        if cols == 2 and rows % 2 == 0 and 2 * panel.shape[3] % panel.shape[4] == 0:
+            return fused(rows, cols, panel, *rest)
+        return plain(panel, *rest)
+
     return jax.shard_map(
         local,
         mesh=mesh,

time: 160 us -> 49.2 us (0.31)
  waiting for transfers between devices: 101 us -> 0 us
  Pallas kernels: 0 us -> 45.3 us
  matrix products: 19.9 us -> 0 us
  local copies, waits for them, and re-layouts: 20 us -> 3.14 us
  between operations: 14 us -> 0.64 us
  other arithmetic: 5.24 us -> 0 us
    all_gather x2 -> x0, waiting for transfers between devices: 94.4 us -> none  [the longest x1 52.7 us: local(): gathered = lax.all_gather(panel, 'row', axis=3, tiled=True)]
    pallas_call x0 -> x1, Pallas kernels: none -> 45.3 us  [fused(): pl.pallas_call(functools.partial(kernel, rows, cols), name='pole_step', o...]
    dot_general x6 -> x0, matrix products: 19.9 us -> none  [the longest x1 4.82 us: local(): jnp.einsum('tab,tbs->tas', tiles[:, 0], chosen[:, 0], preferred_element_t...]
    squeeze x3 -> x0, local copies, waits for them, and re-layouts: 9.15 us -> none  [the longest x2 5.91 us: local(): chosen[:, 1]]
    gather x2 -> x0, local copies, waits for them, and re-layouts: 6.54 us -> none  [local(): fetched = shards[clipped, local_row]]
    reduce_scatter x1 -> x0, waiting for transfers between devices: 6.45 us -> none  [local(): lax.psum_scatter(partial_value, 'col', scatter_dimension=2, tiled=True)]
  transfers between devices with their start and end apart: 3 -> 0, of which waited for: 3 -> 0; matrix products, arithmetic and copies ran while one was open for 1% -> 0% of each run, Pallas kernels for 0% -> 0%
where the time goes in v1:
time: 49.2 us; the launch traced here: 49 us
  Pallas kernels  45.3 us (92%)
  local copies, waits for them, and re-layouts  3.14 us (6%)
  between operations  0.64 us (1%)
    pallas_call x1, Pallas kernels, fused(): pl.pallas_call(functools.partial(kernel, rows, cols), name='pole_step', o...  45.3 us
    unnamed x2, local copies, waits for them, and re-layouts  3.14 us

profile of v1, /device:TPU:0, one launch (start us, length us, event | category | flops | bytes accessed | tf_op | source)
XLA Modules:
  0.0 49.0 jit_solution(10115776479094078221)
XLA Ops:
  0.6 45.3 %pole_step.1 = (f32[2,2,256,128]{3,2,1,0:T(8,128)}, f32[2,512]{1,0:T(2,128)}) custom-call(s32[11]{0:T(128)} %slot_ref.1, s32[11]{0:T(128)} %tcol_ref.1, f32[2]{0:T(128)} %weight_ref.1, bf16[1,8,2,64,128]{4,3,2,1,0:T(8,128)(2,1)} %panel.1, bf16[11,2,512,512]{3,2,1,0:T(8,128)(2,1)} %tiles.1, s32[2,256]{1,0:T(2,128)} %orbitals.1, bf16[2,256,512]{2,1,0:T(8,128)(2,1)} %basis.1, ...), custom_call_target="tpu_custom_call" | custom-call | tf_op jit(solution)/shard_map/pole_step/pallas_call | solution.py:310
  45.9 1.9 %copy.12 = f32[2,2,256,128]{3,2,1,0:T(8,128)} copy(f32[2,2,256,128]{3,2,1,0:T(8,128)} %get-tuple-element.4) | data formatting | bytes 1048576
  47.8 1.3 %copy.13 = f32[2,512]{1,0:T(2,128)} copy(f32[2,512]{1,0:T(2,128)} %get-tuple-element.5) | data formatting | bytes 8192

commit v2 on v1

--- a/solution.py
+++ b/solution.py
@@ -25,7 +25,7 @@
     chunk_count = 2 * depth_z - 1
     chunks = scratch[:chunk_count]
     (tile_buf, basis_buf, super_buf, orb_buf, acc, half_in, pick_hot, basis_hot, send_rows, recv_rows,
-     local_sem, z_send, z_recv, y_send, y_recv, col_sem, orb_send, orb_recv, row_send, row_recv) = scratch[chunk_count:]
+     local_sem, z_send, z_recv, y_send, y_recv, x_send, x_recv, col_sem, orb_send, orb_recv, row_send, row_recv) = scratch[chunk_count:]
     peers = rows * cols
     r = lax.axis_index("row")
     c = lax.axis_index("col")
@@ -40,6 +40,9 @@
     pair = lanes_y * shard_rows
     boxes, orbs = orbitals.shape
     capacity = send_rows.shape[1]
+    pieces = z_send.shape[2]
+    late = pieces // 2
+    step = panel.shape[1] // pieces
 
     def spot(index):
         return {"row": index // cols, "col": index % cols}
@@ -66,63 +69,102 @@
     def down(d):
         return d if d == 0 else depth_z - 1 + d
 
-    def z_copy(kind, d, towards):
-        ident = up if kind == "up" else down
-        side = 0 if kind == "up" else 1
-        src = panel.at[0] if d == 0 else chunks[ident(d)].at[y]
+    idents = {"up": up, "down": down}
+    sides = {"up": 0, "down": 1}
+    other = r + 1 - 2 * y
+    partner = r + lanes_y - 2 * lanes_y * (z % 2)
+
+    def has(kind, d):
+        return z - d >= 0 if kind == "up" else z + d < depth_z
+
+    def can_send(kind):
+        return z + 1 < depth_z if kind == "up" else z >= 1
+
+    def from_partner(kind):
+        return z % 2 == 1 if kind == "up" else z % 2 == 0
+
+    def piece(ref, h):
+        return ref.at[pl.ds(h * step, step)]
+
+    def z_copy(kind, d, h):
+        side = sides[kind]
+        src = panel.at[0] if d == 0 else chunks[idents[kind](d)].at[y]
         return pltpu.make_async_remote_copy(
-            src_ref=src, dst_ref=chunks[ident(d + 1)].at[y],
-            send_sem=z_send.at[side, d], recv_sem=z_recv.at[side, d + 1],
-            device_id={"row": towards}, device_id_type=MESH,
+            src_ref=piece(src, h), dst_ref=piece(chunks[idents[kind](d + 1)].at[y], h),
+            send_sem=z_send.at[side, d, h], recv_sem=z_recv.at[side, d + 1, h],
+            device_id={"row": r + lanes_y if kind == "up" else r - lanes_y}, device_id_type=MESH,
         )
 
-    def z_arrival(kind, d):
-        ident = up if kind == "up" else down
-        side = 0 if kind == "up" else 1
-        dst = chunks[ident(d)].at[y]
+    def z_arrival(kind, d, h):
+        side = sides[kind]
+        dst = piece(chunks[idents[kind](d)].at[y], h)
         return pltpu.make_async_remote_copy(
-            src_ref=dst, dst_ref=dst, send_sem=z_send.at[side, d - 1], recv_sem=z_recv.at[side, d],
-            device_id={"row": r}, device_id_type=MESH,
+            src_ref=dst, dst_ref=dst, send_sem=z_send.at[side, d - 1, h], recv_sem=z_recv.at[side, d, h],
+            device_id={"row": other}, device_id_type=MESH,
         )
 
-    other = r + 1 - 2 * y
-
-    def y_copy(ident):
+    def y_copy(ident, h):
         src = panel.at[0] if ident == 0 else chunks[ident].at[y]
         return pltpu.make_async_remote_copy(
-            src_ref=src, dst_ref=chunks[ident].at[y],
-            send_sem=y_send.at[ident], recv_sem=y_recv.at[ident],
+            src_ref=piece(src, h), dst_ref=piece(chunks[ident].at[y], h),
+            send_sem=y_send.at[ident, h], recv_sem=y_recv.at[ident, h],
             device_id={"row": other}, device_id_type=MESH,
         )
 
-    def y_arrival(ident):
-        dst = chunks[ident].at[1 - y]
+    def y_arrival(ident, h):
+        dst = piece(chunks[ident].at[1 - y], h)
         return pltpu.make_async_remote_copy(
-            src_ref=dst, dst_ref=dst, send_sem=y_send.at[ident], recv_sem=y_recv.at[ident],
+            src_ref=dst, dst_ref=dst, send_sem=y_send.at[ident, h], recv_sem=y_recv.at[ident, h],
             device_id={"row": other}, device_id_type=MESH,
         )
 
-    def has(kind, d):
-        return z - d >= 0 if kind == "up" else z + d < depth_z
-
-    def can_send(kind):
-        return z + 1 < depth_z if kind == "up" else z >= 1
-
-    def next_row(kind):
-        return r + lanes_y if kind == "up" else r - lanes_y
-
-    def forward(kind, d):
-        @pl.when(jnp.logical_and(has(kind, d), can_send(kind)))
-        def _():
-            z_copy(kind, d, next_row(kind)).start()
-
-    def compute(ident, at_z):
+    def extra_copy(kind, h):
+        return pltpu.make_async_remote_copy(
+            src_ref=piece(chunks[0].at[1 - y], h), dst_ref=piece(chunks[idents[kind](1)].at[1 - y], h),
+            send_sem=x_send.at[h], recv_sem=x_recv.at[h],
+            device_id={"row": partner}, device_id_type=MESH,
+        )
+
+    def extra_arrival(kind, h):
+        dst = piece(chunks[idents[kind](1)].at[1 - y], h)
+        return pltpu.make_async_remote_copy(
+            src_ref=dst, dst_ref=dst, send_sem=x_send.at[h], recv_sem=x_recv.at[h],
+            device_id={"row": partner}, device_id_type=MESH,
+        )
+
+    def each(low, high, body):
+        def run(h, carry):
+            body(h)
+            return carry
+        lax.fori_loop(low, high, run, 0)
+
+    def y_forward(kind, d, h, act):
+        ident = idents[kind](d)
+        if d == 1:
+            @pl.when(jnp.logical_or(jnp.logical_not(from_partner(kind)), h < late))
+            def _():
+                act(y_copy(ident, h))
+        else:
+            act(y_copy(ident, h))
+
+    def chunk_ready(kind, d):
+        ident = idents[kind](d)
+        each(0, late if d == 1 else pieces, lambda h: y_arrival(ident, h).wait_recv())
+        if d == 1:
+            @pl.when(from_partner(kind))
+            def _():
+                each(late, pieces, lambda h: extra_arrival(kind, h).wait_recv())
+
+            @pl.when(jnp.logical_not(from_partner(kind)))
+            def _():
+                each(late, pieces, lambda h: y_arrival(ident, h).wait_recv())
+
+    def compute(ident, at_z, first, last, group=1):
         offset = pl.multiple_of(at_z * pair, pair)
         chunk = chunks[ident]
 
-        def one(t, carry):
+        def product(t):
             j = tcol_ref[t]
-            slot = slot_ref[t]
             left = jnp.concatenate(
                 [tile_buf[t, 0, :, pl.ds(offset, pair)], tile_buf[t, 1, :, pl.ds(offset, pair)]], axis=1)
             parts = [chunk[k, j] for k in range(lanes_y)]
@@ -130,16 +172,25 @@
             imag = jnp.concatenate([p[1] for p in parts], axis=0)
             right = jnp.concatenate(
                 [jnp.concatenate([real, imag], axis=1), jnp.concatenate([-imag, real], axis=1)], axis=0)
-            value = jnp.dot(left, right, preferred_element_type=jnp.float32)
+            return jnp.dot(left, right, preferred_element_type=jnp.float32)
+
+        def several(start, count):
+            values = [product(start + k) for k in range(count)]
             for s in range(BR_DEV):
-                acc[s] += jnp.where(slot == s, value, 0.0)
-            return carry
-
-        lax.fori_loop(0, tile_count, one, 0)
-
-    forward("up", 0)
-    forward("down", 0)
-    y_copy(0).start()
+                total = jnp.where(slot_ref[start] == s, values[0], 0.0)
+                for k in range(1, count):
+                    total = total + jnp.where(slot_ref[start + k] == s, values[k], 0.0)
+                acc[s] += total
+
+        if group == 1:
+            each(first, last, lambda t: several(t, 1))
+        else:
+            for start in range(first, last, group):
+                several(start, min(group, last - start))
+
+    def at(kind, d):
+        return z - d if kind == "up" else z + d
+
     orb_copies = []
     for k in range(1, peers):
         target = (me + k) % peers
@@ -149,6 +200,17 @@
         ))
         orb_copies[-1].start()
 
+    def own_z(h):
+        for kind in idents:
+            @pl.when(can_send(kind))
+            def _(kind=kind):
+                z_copy(kind, 0, h).start()
+
+    def own_piece(h):
+        own_z(h)
+        y_copy(0, (h + late) % pieces).start()
+
+    each(0, pieces, own_piece)
     loads[0].wait()
 
     def prepare():
@@ -213,26 +275,72 @@
             hot = jnp.where(arrive == position, 1.0, 0.0).astype(jnp.bfloat16)
             basis_hot[n] = jnp.dot(hot, basis_buf[n], preferred_element_type=jnp.float32).astype(jnp.bfloat16)
 
-    for d in range(1, depth_z + 1):
-        if d < depth_z:
-            for kind, ident in (("up", up(d)), ("down", down(d))):
+    def send_extra(h):
+        y_arrival(0, h).wait_recv()
+        for kind in idents:
+            @pl.when(jnp.logical_not(from_partner(kind)))
+            def _(kind=kind):
+                extra_copy(kind, h).start()
+
+    each(late, pieces, send_extra)
+    prepare()
+    for d in range(1, depth_z):
+        if d == 2:
+            each(0, late, lambda h: y_arrival(0, h).wait_recv())
+            loads[1].wait()
+        if d >= 3:
+            for kind in idents:
+                @pl.when(has(kind, d - 2))
+                def _(kind=kind):
+                    chunk_ready(kind, d - 2)
+
+        final = d >= 3 and d == depth_z - 1
+
+        def arrive_piece(h, d=d, final=final, behind=2):
+            for kind in idents:
                 @pl.when(has(kind, d))
-                def _(kind=kind, ident=ident):
-                    z_arrival(kind, d).wait_recv()
-                    y_copy(ident).start()
-                if d < depth_z - 1:
-                    forward(kind, d)
-        if d == 1:
-            y_arrival(0).wait_recv()
-            loads[1].wait()
-            compute(0, z)
-            prepare()
+                def _(kind=kind):
+                    z_arrival(kind, d, h).wait_recv()
+                    if d < depth_z - 1:
+                        @pl.when(can_send(kind))
+                        def _():
+                            z_copy(kind, d, h).start()
+                    y_forward(kind, d, h, lambda copy: copy.start())
+            first, last = h * tile_count // pieces, (h + 1) * tile_count // pieces
+            if d == 2:
+                compute(0, z, first, last)
+            if final:
+                done = h - (0 if behind == 2 else late)
+                first, last = done * tile_count // late, (done + 1) * tile_count // late
+            if d >= 3:
+                for kind in idents:
+                    @pl.when(has(kind, d if behind == 1 else d - 2))
+                    def _(kind=kind):
+                        compute(idents[kind](d - behind), at(kind, d - behind), first, last)
+
+        if final:
+            each(0, late, arrive_piece)
+            for kind in idents:
+                @pl.when(has(kind, d))
+                def _(kind=kind, d=d):
+                    chunk_ready(kind, d - 1)
+            each(late, pieces, functools.partial(arrive_piece, behind=1))
         else:
-            for kind, ident, at_z in (("up", up(d - 1), z - d + 1), ("down", down(d - 1), z + d - 1)):
-                @pl.when(has(kind, d - 1))
-                def _(ident=ident, at_z=at_z):
-                    y_arrival(ident).wait_recv()
-                    compute(ident, at_z)
+            each(0, pieces, arrive_piece)
+    if depth_z == 2:
+        each(0, late, lambda h: y_arrival(0, h).wait_recv())
+        loads[1].wait()
+        compute(0, z, 0, tile_count)
+    for d in range(max(depth_z - 2, 1), depth_z):
+        for kind in idents:
+            waiting = has(kind, d)
+            if depth_z >= 4 and d == depth_z - 2:
+                waiting = jnp.logical_and(waiting, jnp.logical_not(has(kind, d + 1)))
+
+            @pl.when(waiting)
+            def _(kind=kind, d=d):
+                chunk_ready(kind, d)
+                compute(idents[kind](d), at(kind, d), 0, tile_count, group=4)
 
     mine = pl.ds(pl.multiple_of(c * half, half), half)
     theirs = pl.ds(pl.multiple_of((1 - c) * half, half), half)
@@ -246,8 +354,6 @@
     for s in range(BR_DEV):
         column = -(acc[s, mine, :] + half_in[s])
         real, imag = column[:, :width], column[:, width:]
-        inv_ref[s, 0] = real
-        inv_ref[s, 1] = imag
         density_rows.append((weight_ref[0] * imag + weight_ref[1] * real).astype(jnp.bfloat16))
     density_rows = jnp.concatenate(density_rows, axis=0)
     picked = jnp.dot(pick_hot[...], density_rows, preferred_element_type=jnp.float32).astype(jnp.bfloat16)
@@ -262,6 +368,10 @@
         ))
         row_copies[-1].start()
     recv_rows[me] = send_rows[me]
+    for s in range(BR_DEV):
+        column = -(acc[s, mine, :] + half_in[s])
+        inv_ref[s, 0] = column[:, :width]
+        inv_ref[s, 1] = column[:, width:]
     loads[3].wait()
     for k in range(1, peers):
         origin = (me + peers - k) % peers
@@ -277,17 +387,27 @@
         density_ref[n:n + 1, :] = jnp.sum(
             super_buf[n].astype(jnp.float32) * projected, axis=0, keepdims=True)
 
-    for kind in ("up", "down"):
-        for d in range(depth_z - 1):
-            @pl.when(jnp.logical_and(has(kind, d), can_send(kind)))
-            def _(kind=kind, d=d):
-                z_copy(kind, d, next_row(kind)).wait_send()
-    y_copy(0).wait_send()
-    for d in range(1, depth_z):
-        for kind, ident in (("up", up(d)), ("down", down(d))):
-            @pl.when(has(kind, d))
-            def _(ident=ident):
-                y_copy(ident).wait_send()
+    def sent(h):
+        y_copy(0, h).wait_send()
+        for kind in idents:
+            for d in range(depth_z - 1):
+                @pl.when(jnp.logical_and(has(kind, d), can_send(kind)))
+                def _(kind=kind, d=d):
+                    z_copy(kind, d, h).wait_send()
+            for d in range(1, depth_z):
+                @pl.when(has(kind, d))
+                def _(kind=kind, d=d):
+                    y_forward(kind, d, h, lambda copy: copy.wait_send())
+
+    each(0, pieces, sent)
+
+    def extra_sent(h):
+        for kind in idents:
+            @pl.when(jnp.logical_not(from_partner(kind)))
+            def _(kind=kind):
+                extra_copy(kind, h).wait_send()
+
+    each(late, pieces, extra_sent)
     swap.wait_send()
     for copy in row_copies:
         copy.wait_send()
@@ -302,6 +422,7 @@
     peers = rows * cols
     capacity = 2 * boxes * orbs // peers
     depth_z = rows // 2
+    pieces = blocks // 2
     dma = pltpu.SemaphoreType.DMA
     bf16, f32 = jnp.bfloat16, jnp.float32
     smem = pl.BlockSpec(memory_space=pltpu.SMEM)
@@ -328,10 +449,12 @@
             pltpu.VMEM((peers, capacity, width), bf16),
             pltpu.VMEM((peers, capacity, width), bf16),
             dma((5,)),
-            dma((2, depth_z)),
-            dma((2, depth_z)),
-            dma((2 * depth_z - 1,)),
-            dma((2 * depth_z - 1,)),
+            dma((2, depth_z, pieces)),
+            dma((2, depth_z, pieces)),
+            dma((2 * depth_z - 1, pieces)),
+            dma((2 * depth_z - 1, pieces)),
+            dma((pieces,)),
+            dma((pieces,)),
             dma((2,)),
             dma((peers,)),
             dma((peers,)),
@@ -404,7 +527,7 @@
     rows, cols = mesh.shape["row"], mesh.shape["col"]
 
     def local(panel, *rest):
-        if cols == 2 and rows % 2 == 0 and 2 * panel.shape[3] % panel.shape[4] == 0:
+        if cols == 2 and rows % 4 == 0 and panel.shape[1] % 4 == 0 and 2 * panel.shape[3] % panel.shape[4] == 0:
             return fused(rows, cols, panel, *rest)
         return plain(panel, *rest)
 

time: 49.2 us -> 47.7 us (0.970); the launches traced: 49 us -> 46.9 us
  Pallas kernels: 45.3 us -> 43.1 us
    pallas_call x1, Pallas kernels: 45.3 us -> 43.1 us  [fused(): pl.pallas_call(functools.partial(kernel, rows, cols), name='pole_step', o...]
where the time goes in v2:
time: 47.7 us; the launch traced here: 46.9 us
  Pallas kernels  43.1 us (90%)
  local copies, waits for them, and re-layouts  3.14 us (7%)
  between operations  0.64 us (1%)
    pallas_call x1, Pallas kernels, fused(): pl.pallas_call(functools.partial(kernel, rows, cols), name='pole_step', o...  43.1 us
    unnamed x2, local copies, waits for them, and re-layouts  3.14 us

profile of v2, /device:TPU:0, one launch (start us, length us, event | category | flops | bytes accessed | tf_op | source)
XLA Modules:
  0.0 46.9 jit_solution(907170100978962256)
XLA Ops:
  0.6 43.1 %pole_step.1 = (f32[2,2,256,128]{3,2,1,0:T(8,128)}, f32[2,512]{1,0:T(2,128)}) custom-call(s32[11]{0:T(128)} %slot_ref.1, s32[11]{0:T(128)} %tcol_ref.1, f32[2]{0:T(128)} %weight_ref.1, bf16[1,8,2,64,128]{4,3,2,1,0:T(8,128)(2,1)} %panel.1, bf16[11,2,512,512]{3,2,1,0:T(8,128)(2,1)} %tiles.1, s32[2,256]{1,0:T(2,128)} %orbitals.1, bf16[2,256,512]{2,1,0:T(8,128)(2,1)} %basis.1, ...), custom_call_target="tpu_custom_call" | custom-call | tf_op jit(solution)/shard_map/pole_step/pallas_call | solution.py:431
  43.8 1.9 %copy.12 = f32[2,2,256,128]{3,2,1,0:T(8,128)} copy(f32[2,2,256,128]{3,2,1,0:T(8,128)} %get-tuple-element.4) | data formatting | bytes 1048576
  45.6 1.3 %copy.13 = f32[2,512]{1,0:T(2,128)} copy(f32[2,512]{1,0:T(2,128)} %get-tuple-element.5) | data formatting | bytes 8192
